TPU v7x, 32 devices: a whole 2x2x4 slice. The times are simulated.
32 devices in a mesh: lat: 8 (over z, core), lon: 4 (over y, x).
Axes of the slice: x: 2, y: 2, z: 4, core: 2. Of those that a mesh axis runs over, the one named last changes fastest.
Arguments:
- predicted_state: float32 [1440, 13312], P('lon', 'lat'), may hold values from -24 to 24
- verified_state: float32 [1440, 13312], P('lon', 'lat'), may hold values from -20 to 20
- normal_state: float32 [1440, 13312], P('lon', 'lat'), may hold values from -3 to 3
Outputs:
- energy_curves: float32 [3, 52, 721], replicated
- rms_error: float32 [52], replicated
- anomaly_corr: float32 [52], replicated
All inputs are finite; a program needn't handle non-finite values.
Results may differ from a plain program's by a relative error of at most 0.00005.
Values sent between devices are 32-bit elements; how exact they have to be, the bound alone decides.
A program may use at most 64 MiB of HBM per device.

v0:
```python
import jax
import jax.numpy as jnp
from jax import lax
from jax.sharding import PartitionSpec as P

FIELDS = 52
epsilon = 1e-06


def latitude_weights(lat_index, parallel_number):
    return jnp.cos(jnp.pi * ((lat_index.astype(jnp.float32) + 0.5) / parallel_number - 0.5))


def dft_table(lon_rows, lon_total, wave_count):
    longitudes = jnp.arange(lon_rows, dtype=jnp.int32)
    waves = jnp.arange(wave_count, dtype=jnp.int32)
    phase = longitudes[:, None] * waves[None, :] % lon_total
    angle = 2.0 * jnp.pi / lon_total * phase.astype(jnp.float32)
    return jnp.concatenate([jnp.cos(angle), -jnp.sin(angle)], axis=1)


def transform_columns(stacked, table):
    return lax.dot_general(
        stacked,
        table,
        (((0,), (0,)), ((), ())),
        precision=lax.Precision.HIGHEST,
        preferred_element_type=jnp.float32,
    )


def row_powers(fore_coeffs, true_coeffs, wave_count):
    diff_coeffs = fore_coeffs - true_coeffs

    def square(coeffs):
        return (
            coeffs[:, :wave_count] * coeffs[:, :wave_count]
            + coeffs[:, wave_count:] * coeffs[:, wave_count:]
        )

    return jnp.stack([square(fore_coeffs), square(true_coeffs), square(diff_coeffs)], axis=1)


def local(predicted_state, verified_state, normal_state):
    quantity_labels = FIELDS
    meridian_lines, meridian_number = predicted_state.shape
    parallel_lines = meridian_number // quantity_labels
    parallel_number = parallel_lines * lax.axis_size("lat")
    lon_devices = lax.axis_size("lon")
    lon_total = meridian_lines * lon_devices
    wave_count = lon_total // 2 + 1
    row_share = meridian_number // lon_devices
    lat_first = lax.axis_index("lat") * parallel_lines
    weights = latitude_weights(
        lat_first + jnp.arange(parallel_lines, dtype=jnp.int32), parallel_number
    )
    weight_total = jnp.sum(
        latitude_weights(jnp.arange(parallel_number, dtype=jnp.int32), parallel_number)
    )
    predicted_block = predicted_state.reshape(meridian_lines, parallel_lines, quantity_labels)
    observed_block = verified_state.reshape(meridian_lines, parallel_lines, quantity_labels)
    normal_block = normal_state.reshape(meridian_lines, parallel_lines, quantity_labels)
    mismatch_parts = predicted_block - observed_block
    predicted_anomalies = predicted_block - normal_block
    observed_anomalies = observed_block - normal_block
    broad_layout = weights[None, :, None]
    skill_terms = jnp.stack(
        [
            jnp.sum(broad_layout * mismatch_parts * mismatch_parts, axis=(0, 1)),
            jnp.sum(broad_layout * predicted_anomalies * observed_anomalies, axis=(0, 1)),
            jnp.sum(broad_layout * predicted_anomalies * predicted_anomalies, axis=(0, 1)),
            jnp.sum(broad_layout * observed_anomalies * observed_anomalies, axis=(0, 1)),
        ]
    )
    predicted_meridians = predicted_block.transpose(0, 2, 1).reshape(
        meridian_lines, meridian_number
    )
    true_cols = observed_block.transpose(0, 2, 1).reshape(meridian_lines, meridian_number)
    full_table = dft_table(lon_total, lon_total, wave_count)
    fore_blocks = predicted_meridians.reshape(meridian_lines, lon_devices, row_share)
    true_blocks = true_cols.reshape(meridian_lines, lon_devices, row_share)
    fore_part = lax.all_to_all(fore_blocks, "lon", split_axis=1, concat_axis=0, tiled=True)[:, 0, :]
    true_part = lax.all_to_all(true_blocks, "lon", split_axis=1, concat_axis=0, tiled=True)[:, 0, :]
    items = fore_part.shape[1]
    stacked = jnp.concatenate([fore_part, true_part], axis=1)
    coeffs = transform_columns(stacked, full_table)
    powers = row_powers(coeffs[:items], coeffs[items:], wave_count)
    share_start = lax.axis_index("lon") * row_share
    global_cols = share_start + jnp.arange(row_share, dtype=jnp.int32)
    field_of = global_cols // parallel_lines
    row_weights = latitude_weights(lat_first + global_cols % parallel_lines, parallel_number)
    row_scale = row_weights / (lon_total * lon_total * weight_total)
    weighted = powers.reshape(row_share, 3 * wave_count) * row_scale[:, None]
    field_index = jnp.arange(quantity_labels, dtype=jnp.int32)
    window = min(quantity_labels, row_share // parallel_lines + 2)
    first_field = share_start // parallel_lines
    window_index = jnp.arange(window, dtype=jnp.int32)
    offset = field_of - first_field
    selector = (offset[None, :] == window_index[:, None]).astype(jnp.float32)
    band_sum = jnp.dot(
        selector, weighted, precision=lax.Precision.HIGHEST, preferred_element_type=jnp.float32
    )
    band_sum = lax.psum(band_sum, "lat")
    gathered = lax.all_gather(band_sum, "lon", axis=0, tiled=True)
    slot_index = jnp.arange(lon_devices * window, dtype=jnp.int32)
    slot_field = slot_index // window * row_share // parallel_lines + slot_index % window
    placer = (slot_field[None, :] == field_index[:, None]).astype(jnp.float32)
    summed = jnp.dot(
        placer, gathered, precision=lax.Precision.HIGHEST, preferred_element_type=jnp.float32
    )
    energy_curves = summed.reshape(quantity_labels, 3, wave_count).transpose(1, 0, 2)
    skill_means = lax.psum(skill_terms, ("lat", "lon")) / (lon_total * weight_total)
    rms_error = jnp.sqrt(skill_means[0])
    anomaly_corr = skill_means[1] / jnp.sqrt(
        (skill_means[2] + epsilon) * (skill_means[3] + epsilon)
    )
    return (energy_curves, rms_error, anomaly_corr)


def solution(mesh):
    in_specs = (P("lon", "lat"), P("lon", "lat"), P("lon", "lat"))
    out_specs = (P(), P(), P())
    return jax.shard_map(local, mesh=mesh, in_specs=in_specs, out_specs=out_specs, check_vma=False)
```

profile of v0, /device:TPU:8, one launch (start us, length us, event | category | flops | bytes accessed | tf_op | source)
XLA Modules:
  0.0 275.4 jit_solution(18060614692774121550)
XLA Ops:
  7.2 3.2 %copy.26 = f32[360,1664]{0,1:T(8,128)} copy(f32[360,1664]{1,0:T(8,128)} %param.4) | data formatting | bytes 4792320 | tf_op args[1]
  10.4 2.4 reshape.125
  12.8 1.9 copy.27
  14.8 4.8 %all-to-all-start.1 = ((f32[360,4,416]{0,2,1:T(8,128)}), f32[360,4,416]{0,2,1:T(8,128)}, u32[]{:S(2)}, u32[]{:S(2)}) async-start(f32[360,4,416]{0,2,1:T(8,128)} %bitcast.41), calls=%async_computation.1 | async-start | bytes 5111808 | tf_op jit(solution)/shard_map/all_to_all | solution.py:83
  19.6 2.2 copy.23
  21.7 2.4 reshape.124
  24.2 2.1 copy.24
  26.5 23.2 %all-to-all-done.1 = f32[360,4,416]{0,2,1:T(8,128)} async-done(((f32[360,4,416]{0,2,1:T(8,128)}), f32[360,4,416]{0,2,1:T(8,128)}, u32[]{:S(2)}, u32[]{:S(2)}) %all-to-all-start.1) | async-done | bytes 2396192 | tf_op jit(solution)/shard_map/all_to_all | solution.py:83
  49.7 3.6 %all-to-all-start = ((f32[360,4,416]{0,2,1:T(8,128)}), f32[360,4,416]{0,2,1:T(8,128)S(1)}, u32[]{:S(2)}, u32[]{:S(2)}) async-start(f32[360,4,416]{0,2,1:T(8,128)} %bitcast.39), calls=%async_computation | async-start | bytes 5111808 | tf_op jit(solution)/shard_map/all_to_all | solution.py:82
  53.4 4.3 %fusion.17 = (f32[1664]{0:T(1024)S(1)}, f32[1664]{0:T(1024)S(1)}, f32[1664]{0:T(1024)S(1)}, f32[1664]{0:T(1024)S(1)}) fusion(f32[360,1664]{1,0:T(8,128)} %param.3, f32[360,1664]{1,0:T(8,128)} %param.4, f32[1664]{0:T(1024)S(1)} %mul.171, f32[360,1664]{1,0:T(8,128)} %param.5), kind=kLoop, calls=%fused_computation.26 | loop fusion | flops 8379904 | bytes 7221760 | tf_op jit(solution)/shard_map/reduce_sum | solution.py:69
  60.1 55.8 %psum.15 = f32[4,52]{1,0:T(4,128)S(1)} all-reduce(f32[4,52]{1,0:T(4,128)S(1)} %pad_maximum_fusion.1), channel_id=1, replica_groups=mesh['lat'=8,'lon'=4] {'lat','lon'}, use_global_device_ids=true, to_apply=%region_10.11 | all-reduce | flops 208 | bytes 1664 | tf_op jit(solution)/shard_map/psum | solution.py:112
  116.5 19.7 %sine_negate_fusion = (f32[1440,721]{1,0:T(8,128)}, f32[1440,721]{1,0:T(8,128)}) fusion(), kind=kLoop, calls=%fused_computation.12 | loop fusion | flops 10382400 | bytes 8305920 | tf_op jit(solution)/shard_map/neg | solution.py:19
  136.2 4.8 %copy.28 = f32[4,360,1,416]{1,0,3,2:T(4,128)} copy(f32[4,360,1,416]{1,3,0,2:T(8,128)} %bitcast.7) | data formatting | bytes 4792320 | tf_op jit(solution)/shard_map/all_to_all | solution.py:83
  141.1 4.0 %squeeze.5 = f32[1440,416]{0,1:T(8,128)} reshape(f32[4,360,1,416]{1,0,3,2:T(4,128)} %copy.28) | data formatting | bytes 4792320 | tf_op jit(solution)/shard_map/squeeze | solution.py:83
  145.1 3.1 %copy.25 = f32[4,360,1,416]{1,0,3,2:T(4,128)} copy(f32[4,360,1,416]{1,3,0,2:T(8,128)S(1)} %bitcast.40) | data formatting | bytes 4792320 | tf_op jit(solution)/shard_map/all_to_all | solution.py:82
  148.2 4.2 %squeeze.4 = f32[1440,416]{0,1:T(8,128)} reshape(f32[4,360,1,416]{1,0,3,2:T(4,128)} %copy.25) | data formatting | bytes 4792320 | tf_op jit(solution)/shard_map/squeeze | solution.py:82
  152.4 29.4 %fusion = f32[832,1442]{1,0:T(8,128)S(1)} fusion(f32[1440,721]{1,0:T(8,128)} %get-tuple-element.20, f32[1440,721]{1,0:T(8,128)} %get-tuple-element.21, f32[1440,416]{0,1:T(8,128)S(1)} %copy-done.1, f32[1440,416]{0,1:T(8,128)} %squeeze.4), kind=kOutput, calls=%fused_computation | convolution fusion | flops 20734851072 | bytes 17897216 | tf_op jit(solution)/shard_map/dot_general | solution.py:23
  183.4 2.1 pad_maximum_fusion
  185.5 5.6 %copy.29 = f32[416,3,721]{0,2,1:T(8,128)} copy(f32[416,3,721]{2,0,1:T(8,128)} %pad_maximum_fusion) | data formatting | bytes 7198464 | tf_op jit(solution)/shard_map/stack | solution.py:41
  191.1 4.9 %reshape.126 = f32[416,2163]{0,1:T(8,128)} reshape(f32[416,3,721]{0,2,1:T(8,128)} %copy.29) | data formatting | bytes 7198464 | tf_op jit(solution)/shard_map/reshape | solution.py:93
  196.0 5.2 %fusion.7 = f32[15,2163]{1,0:T(8,128)} fusion(f32[416,2163]{0,1:T(8,128)} %reshape.126, f32[416]{0:T(512)S(1)} %fusion.37, s32[416]{0:T(512)S(1)} %fusion.29), kind=kOutput, calls=%fused_computation.8 | convolution fusion | flops 162871488 | bytes 3732340 | tf_op jit(solution)/shard_map/dot_general | solution.py:100
  201.2 54.4 %all-reduce.2.cloned.1.call-done = f32[15,2163]{1,0:T(8,128)} async-done(((f32[15,2163]{1,0:T(8,128)}), f32[15,2163]{1,0:T(8,128)}) %all-reduce.2.cloned.1.call-update) | async-done | bytes 129796 | tf_op jit(solution)/shard_map/psum | solution.py:103
  255.6 11.1 %all-gather = f32[4,15,2163]{2,1,0:T(8,128)S(1)} all-gather(f32[1,15,2163]{2,1,0:T(8,128)} %bitcast.43), channel_id=1, replica_groups=mesh['lat'=8,'lon'=4] {'lon'}, dimensions={0}, use_global_device_ids=true | all-gather | bytes 648900 | tf_op jit(solution)/shard_map/all_gather | solution.py:104
  267.7 0.9 copy.30
  (31 shorter events, 4.5 us)
Async XLA Ops:
  14.8 4.8 %copy-start = (f32[360,1664]{1,0:T(8,128)S(1)}, f32[360,1664]{1,0:T(8,128)}, u32[]{:S(2)}) copy-start(f32[360,1664]{1,0:T(8,128)} %param.3) | copy-start | bytes 7188484
  14.8 34.9 %all-to-all-start.1 = ((f32[360,4,416]{0,2,1:T(8,128)}), f32[360,4,416]{0,2,1:T(8,128)}, u32[]{:S(2)}, u32[]{:S(2)}) async-start(f32[360,4,416]{0,2,1:T(8,128)} %bitcast.41), calls=%async_computation.1 | async-start | bytes 5111808 | tf_op jit(solution)/shard_map/all_to_all | solution.py:83
  49.7 95.4 %all-to-all-start = ((f32[360,4,416]{0,2,1:T(8,128)}), f32[360,4,416]{0,2,1:T(8,128)S(1)}, u32[]{:S(2)}, u32[]{:S(2)}) async-start(f32[360,4,416]{0,2,1:T(8,128)} %bitcast.39), calls=%async_computation | async-start | bytes 5111808 | tf_op jit(solution)/shard_map/all_to_all | solution.py:82
  53.3 202.3 %all-reduce.2.cloned.1.call-start = ((), (), s32[]{:S(2)}) async-start(), calls=%async_computation.2 | async-start | bytes 278528 | tf_op jit(solution)/shard_map/psum | solution.py:103
  148.2 4.2 %copy-start.1 = (f32[1440,416]{0,1:T(8,128)S(1)}, f32[1440,416]{0,1:T(8,128)}, u32[]{:S(2)}) copy-start(f32[1440,416]{0,1:T(8,128)} %squeeze.5) | copy-start | bytes 7188484
Sparse Core Ops, SparseCore 0:
  201.3 54.3 all-reduce.1
where the time goes:
time: 276 us; the launch traced here: 275 us
  waiting for transfers between devices  77.7 us (28%)
  blocking collectives  66.9 us (24%)
  local copies, waits for them, and re-layouts  42.9 us (16%)
  matrix products  35 us (13%)
  other arithmetic  29 us (11%)
  between operations  15.5 us (6%)
  starting transfers between devices  8.44 us (3%)
    psum x1, blocking collectives, local(): lax.psum(skill_terms, ('lat', 'lon')) / (lon_total * weight_total)  55.8 us
    psum x1, waiting for transfers between devices, local(): band_sum = lax.psum(band_sum, 'lat')  54.4 us
    dot_general x1, matrix products, transform_columns(): lax.dot_general(stacked, table, (((0,), (0,)), ((), ())), precision=lax.P...  29.4 us
    all_to_all x1, waiting for transfers between devices, local(): lax.all_to_all(true_blocks, 'lon', split_axis=1, concat_axis=0, tiled=True)  23.2 us
    neg x1, other arithmetic, dft_table(): return jnp.concatenate([jnp.cos(angle), -jnp.sin(angle)], axis=1)  19.7 us
    all_gather x1, blocking collectives, local(): gathered = lax.all_gather(band_sum, 'lon', axis=0, tiled=True)  11.1 us
    unnamed x8, local copies, waits for them, and re-layouts  6.34 us
    another operation x1, local copies, waits for them, and re-layouts, row_powers(): jnp.stack([square(fore_coeffs), square(true_coeffs), square(diff_coeffs)]...  5.61 us
  transfers between devices with their start and end apart: 3, of which 2 were waited for; matrix products, arithmetic and copies ran while one was open for 15% of the time, Pallas kernels for 0%

commit v1 on v0

--- a/solution.py
+++ b/solution.py
@@ -109,7 +109,10 @@
         placer, gathered, precision=lax.Precision.HIGHEST, preferred_element_type=jnp.float32
     )
     energy_curves = summed.reshape(quantity_labels, 3, wave_count).transpose(1, 0, 2)
-    skill_means = lax.psum(skill_terms, ("lat", "lon")) / (lon_total * weight_total)
+    samples_lay = lambda own_rows, named_axis: jnp.sum(
+        jax.lax.all_gather(own_rows, axis_name=named_axis), axis=0
+    )
+    skill_means = samples_lay(skill_terms, ("lat", "lon")) / (lon_total * weight_total)
     rms_error = jnp.sqrt(skill_means[0])
     anomaly_corr = skill_means[1] / jnp.sqrt(
         (skill_means[2] + epsilon) * (skill_means[3] + epsilon)

time: 276 us -> 299 us (1.083)
  blocking collectives: 66.9 us -> 81.8 us
  waiting for transfers between devices: 77.7 us -> 85.7 us
    all_gather x0 -> x1, blocking collectives: none -> 70.7 us  [local(): jax.lax.all_gather(own_rows, axis_name=named_axis)]
    psum x1 -> x0, blocking collectives: 55.8 us -> none  [local(): lax.psum(skill_terms, ('lat', 'lon')) / (lon_total * weight_total)]
    psum x1, waiting for transfers between devices: 54.4 us -> 62.5 us  [local(): band_sum = lax.psum(band_sum, 'lat')]
  transfers between devices with their start and end apart: 3 -> 3, of which waited for: 2 -> 2; matrix products, arithmetic and copies ran while one was open for 15% -> 14% of each run, Pallas kernels for 0% -> 0%
where the time goes in v1:
time: 299 us; the launch traced here: 298 us
  waiting for transfers between devices  85.7 us (29%)
  blocking collectives  81.8 us (27%)
  local copies, waits for them, and re-layouts  42.9 us (14%)
  matrix products  35 us (12%)
  other arithmetic  29.1 us (10%)
  between operations  15.5 us (5%)
  starting transfers between devices  8.44 us (3%)
    all_gather x1, blocking collectives, local(): jax.lax.all_gather(own_rows, axis_name=named_axis)  70.7 us
    psum x1, waiting for transfers between devices, local(): band_sum = lax.psum(band_sum, 'lat')  62.5 us
    dot_general x1, matrix products, transform_columns(): lax.dot_general(stacked, table, (((0,), (0,)), ((), ())), precision=lax.P...  29.4 us
    all_to_all x1, waiting for transfers between devices, local(): lax.all_to_all(true_blocks, 'lon', split_axis=1, concat_axis=0, tiled=True)  23.2 us
    neg x1, other arithmetic, dft_table(): return jnp.concatenate([jnp.cos(angle), -jnp.sin(angle)], axis=1)  19.7 us
    all_gather x1, blocking collectives, local(): gathered = lax.all_gather(band_sum, 'lon', axis=0, tiled=True)  11.1 us
    unnamed x8, local copies, waits for them, and re-layouts  6.34 us
  transfers between devices with their start and end apart: 3, of which 2 were waited for; matrix products, arithmetic and copies ran while one was open for 14% of the time, Pallas kernels for 0%

profile of v1, /device:TPU:8, one launch (start us, length us, event | category | flops | bytes accessed | tf_op | source)
XLA Modules:
  0.0 298.4 jit_solution(9999908452201834138)
XLA Ops:
  7.2 3.2 %copy.26 = f32[360,1664]{0,1:T(8,128)} copy(f32[360,1664]{1,0:T(8,128)} %param.4) | data formatting | bytes 4792320 | tf_op args[1]
  10.4 2.4 reshape.125
  12.8 1.9 copy.27
  14.8 4.8 %all-to-all-start.1 = ((f32[360,4,416]{0,2,1:T(8,128)}), f32[360,4,416]{0,2,1:T(8,128)}, u32[]{:S(2)}, u32[]{:S(2)}) async-start(f32[360,4,416]{0,2,1:T(8,128)} %bitcast.43), calls=%async_computation.1 | async-start | bytes 5111808 | tf_op jit(solution)/shard_map/all_to_all | solution.py:83
  19.6 2.2 copy.23
  21.7 2.4 reshape.124
  24.2 2.1 copy.24
  26.5 23.2 %all-to-all-done.1 = f32[360,4,416]{0,2,1:T(8,128)} async-done(((f32[360,4,416]{0,2,1:T(8,128)}), f32[360,4,416]{0,2,1:T(8,128)}, u32[]{:S(2)}, u32[]{:S(2)}) %all-to-all-start.1) | async-done | bytes 2396192 | tf_op jit(solution)/shard_map/all_to_all | solution.py:83
  49.7 3.6 %all-to-all-start = ((f32[360,4,416]{0,2,1:T(8,128)}), f32[360,4,416]{0,2,1:T(8,128)S(1)}, u32[]{:S(2)}, u32[]{:S(2)}) async-start(f32[360,4,416]{0,2,1:T(8,128)} %bitcast.41), calls=%async_computation | async-start | bytes 5111808 | tf_op jit(solution)/shard_map/all_to_all | solution.py:82
  53.4 4.3 %fusion.17 = (f32[1664]{0:T(1024)S(1)}, f32[1664]{0:T(1024)S(1)}, f32[1664]{0:T(1024)S(1)}, f32[1664]{0:T(1024)S(1)}) fusion(f32[360,1664]{1,0:T(8,128)} %param.3, f32[360,1664]{1,0:T(8,128)} %param.4, f32[1664]{0:T(1024)S(1)} %mul.171, f32[360,1664]{1,0:T(8,128)} %param.5), kind=kLoop, calls=%fused_computation.26 | loop fusion | flops 8379904 | bytes 7221760 | tf_op jit(solution)/shard_map/reduce_sum | solution.py:69
  58.1 70.7 %all-gather.2 = f32[32,4,52]{2,1,0:T(4,128)S(1)} all-gather(f32[1,4,52]{2,1,0:T(4,128)S(1)} %maximum_bitcast_fusion), channel_id=2, replica_groups=mesh['lat'=8,'lon'=4] {'lat','lon'}, dimensions={0}, use_global_device_ids=true | all-gather | bytes 27456 | tf_op jit(solution)/shard_map/all_gather | solution.py:113
  131.5 19.7 %sine_negate_fusion = (f32[1440,721]{1,0:T(8,128)}, f32[1440,721]{1,0:T(8,128)}) fusion(), kind=kLoop, calls=%fused_computation.12 | loop fusion | flops 10382400 | bytes 8305920 | tf_op jit(solution)/shard_map/neg | solution.py:19
  151.2 4.8 %copy.28 = f32[4,360,1,416]{1,0,3,2:T(4,128)} copy(f32[4,360,1,416]{1,3,0,2:T(8,128)} %bitcast.7) | data formatting | bytes 4792320 | tf_op jit(solution)/shard_map/all_to_all | solution.py:83
  156.0 4.0 %squeeze.5 = f32[1440,416]{0,1:T(8,128)} reshape(f32[4,360,1,416]{1,0,3,2:T(4,128)} %copy.28) | data formatting | bytes 4792320 | tf_op jit(solution)/shard_map/squeeze | solution.py:83
  160.1 3.1 %copy.25 = f32[4,360,1,416]{1,0,3,2:T(4,128)} copy(f32[4,360,1,416]{1,3,0,2:T(8,128)S(1)} %bitcast.42) | data formatting | bytes 4792320 | tf_op jit(solution)/shard_map/all_to_all | solution.py:82
  163.2 4.2 %squeeze.4 = f32[1440,416]{0,1:T(8,128)} reshape(f32[4,360,1,416]{1,0,3,2:T(4,128)} %copy.25) | data formatting | bytes 4792320 | tf_op jit(solution)/shard_map/squeeze | solution.py:82
  167.4 29.4 %fusion = f32[832,1442]{1,0:T(8,128)S(1)} fusion(f32[1440,721]{1,0:T(8,128)} %get-tuple-element.20, f32[1440,721]{1,0:T(8,128)} %get-tuple-element.21, f32[1440,416]{0,1:T(8,128)S(1)} %copy-done.1, f32[1440,416]{0,1:T(8,128)} %squeeze.4), kind=kOutput, calls=%fused_computation | convolution fusion | flops 20734851072 | bytes 17897216 | tf_op jit(solution)/shard_map/dot_general | solution.py:23
  198.4 2.1 pad_maximum_fusion
  200.5 5.6 %copy.29 = f32[416,3,721]{0,2,1:T(8,128)} copy(f32[416,3,721]{2,0,1:T(8,128)} %pad_maximum_fusion) | data formatting | bytes 7198464 | tf_op jit(solution)/shard_map/stack | solution.py:41
  206.1 4.9 %reshape.126 = f32[416,2163]{0,1:T(8,128)} reshape(f32[416,3,721]{0,2,1:T(8,128)} %copy.29) | data formatting | bytes 7198464 | tf_op jit(solution)/shard_map/reshape | solution.py:93
  210.9 5.2 %fusion.7 = f32[15,2163]{1,0:T(8,128)} fusion(f32[416,2163]{0,1:T(8,128)} %reshape.126, f32[416]{0:T(512)S(1)} %fusion.37, s32[416]{0:T(512)S(1)} %fusion.29), kind=kOutput, calls=%fused_computation.8 | convolution fusion | flops 162871488 | bytes 3732340 | tf_op jit(solution)/shard_map/dot_general | solution.py:100
  216.2 62.5 %all-reduce.2.cloned.1.call-done = f32[15,2163]{1,0:T(8,128)} async-done(((f32[15,2163]{1,0:T(8,128)}), f32[15,2163]{1,0:T(8,128)}) %all-reduce.2.cloned.1.call-update) | async-done | bytes 129796 | tf_op jit(solution)/shard_map/psum | solution.py:103
  278.7 11.1 %all-gather.1 = f32[4,15,2163]{2,1,0:T(8,128)S(1)} all-gather(f32[1,15,2163]{2,1,0:T(8,128)} %bitcast.45), channel_id=1, replica_groups=mesh['lat'=8,'lon'=4] {'lon'}, dimensions={0}, use_global_device_ids=true | all-gather | bytes 648900 | tf_op jit(solution)/shard_map/all_gather | solution.py:104
  290.7 0.9 copy.30
  (32 shorter events, 4.6 us)
Async XLA Ops:
  14.8 4.8 %copy-start = (f32[360,1664]{1,0:T(8,128)S(1)}, f32[360,1664]{1,0:T(8,128)}, u32[]{:S(2)}) copy-start(f32[360,1664]{1,0:T(8,128)} %param.3) | copy-start | bytes 7188484
  14.8 34.9 %all-to-all-start.1 = ((f32[360,4,416]{0,2,1:T(8,128)}), f32[360,4,416]{0,2,1:T(8,128)}, u32[]{:S(2)}, u32[]{:S(2)}) async-start(f32[360,4,416]{0,2,1:T(8,128)} %bitcast.43), calls=%async_computation.1 | async-start | bytes 5111808 | tf_op jit(solution)/shard_map/all_to_all | solution.py:83
  49.7 110.4 %all-to-all-start = ((f32[360,4,416]{0,2,1:T(8,128)}), f32[360,4,416]{0,2,1:T(8,128)S(1)}, u32[]{:S(2)}, u32[]{:S(2)}) async-start(f32[360,4,416]{0,2,1:T(8,128)} %bitcast.41), calls=%async_computation | async-start | bytes 5111808 | tf_op jit(solution)/shard_map/all_to_all | solution.py:82
  53.3 225.4 %all-reduce.2.cloned.1.call-start = ((), (), s32[]{:S(2)}) async-start(), calls=%async_computation.2 | async-start | bytes 278528 | tf_op jit(solution)/shard_map/psum | solution.py:103
  163.2 4.2 %copy-start.1 = (f32[1440,416]{0,1:T(8,128)S(1)}, f32[1440,416]{0,1:T(8,128)}, u32[]{:S(2)}) copy-start(f32[1440,416]{0,1:T(8,128)} %squeeze.5) | copy-start | bytes 7188484
Sparse Core Ops, SparseCore 0:
  216.3 62.3 all-reduce.1
